TPU v7x, 256 devices: a whole 4x4x8 slice. The times are simulated.
256 devices in a mesh: seq: 16 (over x, y), head: 16 (over z, core).
Axes of the slice: x: 4, y: 4, z: 8, core: 2. Of those that a mesh axis runs over, the one named last changes fastest.
Arguments:
- queries: bfloat16 [16384, 4096], P('seq', 'head'), may hold values from -100 to 100
- states: bfloat16 [4096, 8192], P('seq', 'head'), may hold values from -6 to 6
- key_weight: bfloat16 [8192, 4096], P(None, 'head'), may hold values from -0.0625 to 0.0625
- value_weight: bfloat16 [8192, 4096], P(None, 'head'), may hold values from -0.0625 to 0.0625
- neighbour_ids: int32 [256, 2], P('seq'), may hold values from 0 to 31, all different within a row
- out_grad: bfloat16 [16384, 4096], P('seq', 'head'), may hold values from -4 to 4
Outputs:
- context: bfloat16 [16384, 4096], P('seq', 'head')
- query_grad: bfloat16 [16384, 4096], P('seq', 'head')
- key_weight_grad: float32 [8192, 4096], P('seq', 'head')
- value_weight_grad: float32 [8192, 4096], P('seq', 'head')
Inputs may be any that keep to these rules, and one draw needn't show every extreme that they name: `neighbour_ids`: each span names 2 different pool blocks, and every block is named by some span.
All inputs are finite; a program needn't handle non-finite values.
Results may differ from a plain program's by a relative error of at most 0.04.
Values may be sent and summed in bfloat16 or wider, within the bound.
A program may use at most 128 MiB of HBM per device.

v0:
```python
import math
import jax
import jax.numpy as jnp
from jax import lax
from jax.sharding import PartitionSpec as P

HD = 128
SPAN = 64
NBR = 128
TOPN = 2


def local(queries, states, key_weight, value_weight, neighbour_ids, out_grad):
    head_cols = queries.shape[1]
    heads_here = head_cols // HD
    own_rows = states.shape[0]
    seq_count = lax.axis_size("seq")
    pool_total = own_rows * seq_count
    block_count = pool_total // NBR
    span_count = neighbour_ids.shape[0]
    score_scale = 1.0 / math.sqrt(HD)
    full_states = lax.all_gather(states, "head", axis=1, tiled=True)
    own_keys = jnp.dot(full_states, key_weight, preferred_element_type=jnp.float32).astype(
        jnp.bfloat16
    )
    own_values = jnp.dot(full_states, value_weight, preferred_element_type=jnp.float32).astype(
        jnp.bfloat16
    )
    pool_keys, pool_values = (
        lax.all_gather(own_keys, "seq", axis=0, tiled=True),
        lax.all_gather(own_values, "seq", axis=0, tiled=True),
    )
    key_rows = pool_keys.reshape(block_count, NBR, head_cols)[neighbour_ids]
    key_rows = key_rows.reshape(span_count, TOPN * NBR, heads_here, HD)
    value_rows = pool_values.reshape(block_count, NBR, head_cols)[neighbour_ids]
    value_rows = value_rows.reshape(span_count, TOPN * NBR, heads_here, HD)
    queries_here = queries.reshape(span_count, SPAN, heads_here, HD)
    grad_here = out_grad.reshape(span_count, SPAN, heads_here, HD)
    scores = (
        jnp.einsum("cqhd,ckhd->chqk", queries_here, key_rows, preferred_element_type=jnp.float32)
        * score_scale
    )
    soft_weights = jax.nn.softmax(scores, axis=-1)
    weights_low = soft_weights.astype(jnp.bfloat16)
    context = jnp.einsum(
        "chqk,ckhd->cqhd", weights_low, value_rows, preferred_element_type=jnp.float32
    ).astype(jnp.bfloat16)
    prob_grad = jnp.einsum(
        "cqhd,ckhd->chqk", grad_here, value_rows, preferred_element_type=jnp.float32
    )
    row_delta = jnp.sum(soft_weights * prob_grad, axis=-1, keepdims=True)
    score_grad = (soft_weights * (prob_grad - row_delta) * score_scale).astype(jnp.bfloat16)
    query_grad = jnp.einsum(
        "chqk,ckhd->cqhd", score_grad, key_rows, preferred_element_type=jnp.float32
    ).astype(jnp.bfloat16)
    key_part = jnp.einsum(
        "chqk,cqhd->ckhd", score_grad, queries_here, preferred_element_type=jnp.float32
    )
    value_part = jnp.einsum(
        "chqk,cqhd->ckhd", weights_low, grad_here, preferred_element_type=jnp.float32
    )
    both_parts = jnp.concatenate(
        [
            key_part.reshape(span_count * TOPN, NBR, head_cols),
            value_part.reshape(span_count * TOPN, NBR, head_cols),
        ],
        axis=2,
    )
    parts_high = both_parts.astype(jnp.bfloat16)
    parts_rest = (both_parts - parts_high.astype(jnp.float32)).astype(jnp.bfloat16)
    flat_ids = neighbour_ids.reshape(-1)
    block_range = jnp.arange(own_rows * lax.axis_size("seq") // NBR, dtype=jnp.int32)
    block_picks = (flat_ids[:, None] == block_range[None, :]).astype(jnp.bfloat16)
    summed_rows = jnp.einsum(
        "jb,jrc->brc", block_picks, parts_high, preferred_element_type=jnp.float32
    )
    summed_rows = summed_rows + jnp.einsum(
        "jb,jrc->brc", block_picks, parts_rest, preferred_element_type=jnp.float32
    )
    own_grad = lax.psum_scatter(
        summed_rows.reshape(own_rows * lax.axis_size("seq"), 2 * head_cols).astype(jnp.bfloat16),
        "seq",
        scatter_dimension=0,
        tiled=True,
    )
    weight_grads_all = lax.psum_scatter(
        jnp.einsum("rf,rc->fc", full_states, own_grad, preferred_element_type=jnp.float32).astype(
            jnp.bfloat16
        ),
        "seq",
        scatter_dimension=0,
        tiled=True,
    ).astype(jnp.float32)
    return (
        context.reshape(span_count * SPAN, head_cols),
        query_grad.reshape(span_count * SPAN, head_cols),
        weight_grads_all[:, :head_cols],
        weight_grads_all[:, head_cols:],
    )


def solution(mesh):
    in_specs = (
        P("seq", "head"),
        P("seq", "head"),
        P(None, "head"),
        P(None, "head"),
        P("seq", None),
        P("seq", "head"),
    )
    out_specs = (P("seq", "head"), P("seq", "head"), P("seq", "head"), P("seq", "head"))
    return jax.shard_map(local, mesh=mesh, in_specs=in_specs, out_specs=out_specs, check_vma=False)
```

profile of v0, /device:TPU:2, one launch (start us, length us, event | category | flops | bytes accessed | tf_op | source)
XLA Modules:
  0.0 437.8 jit_solution(14851394914533141190)
XLA Ops:
  7.9 47.0 %all-gather.4.cloned.1.call-done = bf16[256,8192]{1,0:T(8,128)(2,1)} async-done(((bf16[256,512]{1,0:T(8,128)(2,1)}), bf16[256,8192]{1,0:T(8,128)(2,1)}) %all-gather.4.cloned.1.call-update) | async-done | bytes 4194320 | tf_op jit(solution)/shard_map/all_gather | solution.py:22
  55.0 5.4 %convolution_convert_fusion.1 = bf16[256,256]{1,0:T(8,128)(2,1)} fusion(bf16[256,8192]{1,0:T(8,128)(2,1)} %all-gather.4.cloned.1.call-done, bf16[8192,256]{1,0:T(8,128)(2,1)} %param.8), kind=kOutput, calls=%fused_computation.36 | convolution fusion | flops 1073807360 | bytes 8519680 | tf_op jit(solution)/shard_map/dot_general | solution.py:23
  60.4 5.4 %convolution_convert_fusion.2 = bf16[256,256]{1,0:T(8,128)(2,1)} fusion(bf16[256,8192]{1,0:T(8,128)(2,1)} %all-gather.4.cloned.1.call-done, bf16[8192,256]{1,0:T(8,128)(2,1)} %param.9), kind=kOutput, calls=%fused_computation.37 | convolution fusion | flops 1073807360 | bytes 8519680 | tf_op jit(solution)/shard_map/dot_general | solution.py:26
  66.8 41.9 %all-gather.8.cloned.1.call-done = bf16[4096,256]{1,0:T(8,128)(2,1)} async-done(((bf16[256,256]{1,0:T(8,128)(2,1)}), bf16[4096,256]{1,0:T(8,128)(2,1)}) %all-gather.8.cloned.1.call-update) | async-done | bytes 2097168 | tf_op jit(solution)/shard_map/all_gather | solution.py:30
  108.7 3.6 gather_fusion.1
  112.3 2.5 reshape.78
  114.9 46.3 %all-gather.6.cloned.1.call-done = bf16[4096,256]{1,0:T(8,128)(2,1)} async-done(((bf16[256,256]{1,0:T(8,128)(2,1)}), bf16[4096,256]{1,0:T(8,128)(2,1)}) %all-gather.6.cloned.1.call-update) | async-done | bytes 2097168 | tf_op jit(solution)/shard_map/all_gather | solution.py:31
  161.1 3.6 gather_fusion
  164.7 4.0 reshape.77
  169.6 1.8 fusion.64
  172.7 2.2 fusion.19
  174.8 8.5 %convolution_bitcast_fusion = f32[16,256,2,128]{3,1,2,0:T(8,128)} fusion(bf16[16,64,2,128]{3,2,1,0:T(2,128)(2,1)S(1)} %reshape.50, f32[16,2,64]{2,1,0:T(2,128)S(1)} %get-tuple-element.18, f32[16,2,256,64]{2,3,1,0:T(8,128)} %copy-done.3), kind=kOutput, calls=%fused_computation.12 | convolution fusion | flops 136841472 | bytes 6823936 | tf_op jit(solution)/shard_map/chqk,cqhd->ckhd/dot_general | solution.py:59
  183.3 17.6 %convolution_bitcast_fusion.1 = f32[16,256,2,128]{3,1,2,0:T(8,128)} fusion(f32[16,2,256,64]{2,3,1,0:T(8,128)} %fusion.19, bf16[16,64,2,128]{3,2,1,0:T(2,128)(2,1)S(1)} %reshape.48, f32[16,2,64,256]{3,2,1,0:T(8,128)} %get-tuple-element.19, f32[16,2,64]{2,1,0:T(2,128)S(1)} %get-tuple-element.18), kind=kOutput, calls=%fused_computation.13 | convolution fusion | flops 137890048 | bytes 8921088 | tf_op jit(solution)/shard_map/chqk,cqhd->ckhd/dot_general | solution.py:56
  200.9 5.5 %copy.50 = f32[16,256,2,128]{1,0,3,2:T(8,128)} copy(f32[16,256,2,128]{3,1,2,0:T(8,128)} %convolution_bitcast_fusion.1) | data formatting | bytes 8388608 | tf_op jit(solution)/shard_map/chqk,cqhd->ckhd/transpose | solution.py:56
  206.4 4.7 %reshape.52 = f32[32,128,256]{1,0,2:T(8,128)} reshape(f32[16,256,2,128]{1,0,3,2:T(8,128)} %copy.50) | data formatting | bytes 8388608 | tf_op jit(solution)/shard_map/reshape | solution.py:64
  211.1 5.6 %copy.53 = f32[32,128,256]{2,0,1:T(8,128)} copy(f32[32,128,256]{1,0,2:T(8,128)} %reshape.52) | data formatting | bytes 8388608 | tf_op jit(solution)/shard_map/reshape | solution.py:64
  216.7 5.5 %copy.52 = f32[16,256,2,128]{1,0,3,2:T(8,128)} copy(f32[16,256,2,128]{3,1,2,0:T(8,128)} %convolution_bitcast_fusion) | data formatting | bytes 8388608 | tf_op jit(solution)/shard_map/chqk,cqhd->ckhd/transpose | solution.py:59
  222.2 4.7 %reshape.53 = f32[32,128,256]{1,0,2:T(8,128)} reshape(f32[16,256,2,128]{1,0,3,2:T(8,128)} %copy.52) | data formatting | bytes 8388608 | tf_op jit(solution)/shard_map/reshape | solution.py:65
  226.9 5.6 %copy.54 = f32[32,128,256]{2,0,1:T(8,128)} copy(f32[32,128,256]{1,0,2:T(8,128)} %reshape.53) | data formatting | bytes 8388608 | tf_op jit(solution)/shard_map/reshape | solution.py:65
  232.5 4.8 %fusion.4 = f32[32,128,512]{2,0,1:T(8,128)S(1)} fusion(f32[32,128,256]{2,0,1:T(8,128)} %copy.54, f32[32,128,256]{2,0,1:T(8,128)} %copy.53, s32[32]{0:T(128)S(1)} %eq.15), kind=kOutput, calls=%fused_computation.10 | convolution fusion | flops 142607360 | bytes 16777344 | tf_op jit(solution)/shard_map/jb,jrc->brc/dot_general | solution.py:74
  237.4 1.1 copy-done.1
  238.5 2.8 add_convert_fusion
  241.3 6.5 %copy.55 = bf16[32,128,512]{2,1,0:T(8,128)(2,1)} copy(bf16[32,128,512]{2,0,1:T(8,128)(2,1)} %add_convert_fusion) | data formatting | bytes 8388608 | tf_op jit(solution)/shard_map/convert_element_type | solution.py:81
  247.8 82.2 %reduce-scatter.3.cloned.1.call-done = bf16[256,512]{1,0:T(8,128)(2,1)} async-done(((bf16[4096,512]{1,0:T(8,128)(2,1)}), bf16[256,512]{1,0:T(8,128)(2,1)}) %reduce-scatter.3.cloned.1.call-update) | async-done | bytes 262160 | tf_op jit(solution)/shard_map/reduce_scatter | solution.py:80
  330.0 7.9 %fusion.2 = bf16[8192,512]{0,1:T(8,128)(2,1)} fusion(bf16[256,512]{1,0:T(8,128)(2,1)} %reduce-scatter.3.cloned.1.call-done, bf16[256,8192]{1,0:T(8,128)(2,1)} %all-gather.4.cloned.1.call-done), kind=kOutput, calls=%fused_computation.5 | convolution fusion | flops 2151677952 | bytes 12845056 | tf_op jit(solution)/shard_map/rf,rc->fc/dot_general | solution.py:87
  337.9 14.7 %fusion.29 = bf16[16,64,2,128]{3,1,2,0:T(8,128)(2,1)S(1)} fusion(bf16[16,256,2,128]{3,2,1,0:T(2,128)(2,1)S(1)} %reshape.78, f32[16,2,256,64]{2,3,1,0:T(8,128)} %fusion.19, f32[16,2,64,256]{3,2,1,0:T(8,128)} %get-tuple-element.19, f32[16,2,64]{2,1,0:T(2,128)S(1)} %get-tuple-element.18), kind=kOutput, calls=%fused_computation.34 | convolution fusion | flops 138152192 | bytes 6823936 | tf_op jit(solution)/shard_map/chqk,ckhd->cqhd/dot_general | solution.py:53
  353.2 6.6 %fusion.32 = bf16[16,64,2,128]{3,1,2,0:T(8,128)(2,1)S(1)} fusion(bf16[16,256,2,128]{3,2,1,0:T(2,128)(2,1)} %reshape.77, f32[16,2,64]{2,1,0:T(2,128)S(1)} %get-tuple-element.18, f32[16,2,256,64]{2,3,1,0:T(8,128)} %copy-done.3), kind=kOutput, calls=%fused_computation.35 | convolution fusion | flops 137103616 | bytes 4726784 | tf_op jit(solution)/shard_map/chqk,ckhd->cqhd/dot_general | solution.py:45
  360.3 1.1 copy_bitcast_fusion
  361.4 66.7 %reduce-scatter.5.cloned.1.call-done = bf16[512,512]{0,1:T(8,128)(2,1)} async-done(((bf16[8192,512]{0,1:T(8,128)(2,1)}), bf16[512,512]{0,1:T(8,128)(2,1)}) %reduce-scatter.5.cloned.1.call-update) | async-done | bytes 524304 | tf_op jit(solution)/shard_map/reduce_scatter | solution.py:86
  428.1 1.1 fusion.63
  429.3 1.0 copy.57
  430.3 1.0 copy.56
  (34 shorter events, 5.0 us)
Async XLA Ops:
  7.2 47.8 %all-gather.4.cloned.1.call-start = ((), (), s32[]{:S(2)}) async-start(), calls=%async_computation.2 | async-start | bytes 4456448 | tf_op jit(solution)/shard_map/all_gather | solution.py:22
  7.9 100.8 %all-gather.8.cloned.1.call-start = ((), (), s32[]{:S(2)}) async-start(), calls=%async_computation.4 | async-start | bytes 2228224 | tf_op jit(solution)/shard_map/all_gather | solution.py:30
  60.4 5.8 %copy-start.6 = (s32[16,2]{0,1:T(2,128)S(1)}, s32[16,2]{0,1:T(2,128)}, u32[]{:S(2)}) copy-start(s32[16,2]{0,1:T(2,128)} %param.10) | copy-start | bytes 388
  60.4 6.1 %copy-start.4 = (bf16[1024,256]{1,0:T(8,128)(2,1)S(1)}, bf16[1024,256]{1,0:T(8,128)(2,1)}, u32[]{:S(2)}) copy-start(bf16[1024,256]{1,0:T(8,128)(2,1)} %param.6) | copy-start | bytes 1572868
  60.4 6.3 %copy-start.5 = (bf16[1024,256]{1,0:T(8,128)(2,1)S(1)}, bf16[1024,256]{1,0:T(8,128)(2,1)}, u32[]{:S(2)}) copy-start(bf16[1024,256]{1,0:T(8,128)(2,1)} %param.11) | copy-start | bytes 1572868
  60.4 100.7 %all-gather.6.cloned.1.call-start = ((), (), s32[]{:S(2)}) async-start(), calls=%async_computation.3 | async-start | bytes 2228224 | tf_op jit(solution)/shard_map/all_gather | solution.py:31
  65.9 264.1 %reduce-scatter.3.cloned.1.call-start = ((), (), s32[]{:S(2)}) async-start(), calls=%async_computation.5 | async-start | bytes 4456448 | tf_op jit(solution)/shard_map/reduce_scatter | solution.py:80
  169.5 2.1 copy-start.3
  169.5 3.1 copy-start.2
  232.5 4.8 %copy-start = (f32[32,128,256]{2,0,1:T(8,128)S(1)}, f32[32,128,256]{2,0,1:T(8,128)}, u32[]{:S(2)}) copy-start(f32[32,128,256]{2,0,1:T(8,128)} %copy.53) | copy-start | bytes 12582916
  232.5 5.9 %copy-start.1 = (f32[32,128,256]{2,0,1:T(8,128)S(1)}, f32[32,128,256]{2,0,1:T(8,128)}, u32[]{:S(2)}) copy-start(f32[32,128,256]{2,0,1:T(8,128)} %copy.54) | copy-start | bytes 12582916
  247.8 180.4 %reduce-scatter.5.cloned.1.call-start = ((), (), s32[]{:S(2)}) async-start(), calls=%async_computation.6 | async-start | bytes 8912896 | tf_op jit(solution)/shard_map/reduce_scatter | solution.py:86
Sparse Core Ops, SparseCore 0:
  9.8 45.0 all-gather.3
  60.5 48.1 all-gather.7
  111.7 49.3 all-gather.5
  247.9 82.0 reduce-scatter.2
  338.0 90.0 reduce-scatter.4
where the time goes:
time: 439 us; the launch traced here: 438 us
  waiting for transfers between devices  285 us (65%)
  matrix products  76.7 us (17%)
  local copies, waits for them, and re-layouts  60.1 us (14%)
  between operations  13.9 us (3%)
    reduce_scatter x1, waiting for transfers between devices, local(): lax.psum_scatter(summed_rows.reshape(own_rows * lax.axis_size('seq'), 2 *...  82.2 us
    reduce_scatter x1, waiting for transfers between devices, local(): lax.psum_scatter(jnp.einsum('rf,rc->fc', full_states, own_grad, preferred...  66.7 us
    all_gather x1, waiting for transfers between devices, local(): full_states = lax.all_gather(states, 'head', axis=1, tiled=True)  47 us
    all_gather x1, waiting for transfers between devices, local(): lax.all_gather(own_values, 'seq', axis=0, tiled=True)  46.3 us
    all_gather x1, waiting for transfers between devices, local(): lax.all_gather(own_keys, 'seq', axis=0, tiled=True)  41.9 us
    dot_general x1, matrix products, local(): jnp.einsum('chqk,cqhd->ckhd', score_grad, queries_here, preferred_element...  17.6 us
    dot_general x1, matrix products, local(): jnp.einsum('chqk,ckhd->cqhd', score_grad, key_rows, preferred_element_typ...  14.7 us
    reshape x2, local copies, waits for them, and re-layouts, local(): key_part.reshape(span_count * TOPN, NBR, head_cols)  10.3 us
  transfers between devices with their start and end apart: 5, of which 5 were waited for; matrix products, arithmetic and copies ran while one was open for 8% of the time, Pallas kernels for 0%

commit v1 on v0

--- a/solution.py
+++ b/solution.py
@@ -10,6 +10,11 @@
 TOPN = 2
 
 
+def gather_by_exchange(x, axis, dim):
+    copies = jnp.concatenate([x] * lax.axis_size(axis), axis=dim)
+    return lax.all_to_all(copies, axis, dim, dim, tiled=True)
+
+
 def local(queries, states, key_weight, value_weight, neighbour_ids, out_grad):
     head_cols = queries.shape[1]
     heads_here = head_cols // HD
@@ -19,7 +24,7 @@
     block_count = pool_total // NBR
     span_count = neighbour_ids.shape[0]
     score_scale = 1.0 / math.sqrt(HD)
-    full_states = lax.all_gather(states, "head", axis=1, tiled=True)
+    full_states = gather_by_exchange(states, "head", 1)
     own_keys = jnp.dot(full_states, key_weight, preferred_element_type=jnp.float32).astype(
         jnp.bfloat16
     )

time: 439 us -> 508 us (1.16)
  blocking collectives: 0 us -> 103 us
  waiting for transfers between devices: 285 us -> 236 us
  local copies, waits for them, and re-layouts: 60.1 us -> 74 us
    all_to_all x0 -> x1, blocking collectives: none -> 103 us  [gather_by_exchange(): return lax.all_to_all(copies, axis, dim, dim, tiled=True)]
    all_gather x1 -> x0, waiting for transfers between devices: 47 us -> none  [local(): full_states = lax.all_gather(states, 'head', axis=1, tiled=True)]
    all_to_all x0 -> x2, local copies, waits for them, and re-layouts: none -> 12.8 us  [gather_by_exchange(): return lax.all_to_all(copies, axis, dim, dim, tiled=True)]
  transfers between devices with their start and end apart: 5 -> 4, of which waited for: 5 -> 4; matrix products, arithmetic and copies ran while one was open for 8% -> 7% of each run, Pallas kernels for 0% -> 0%
where the time goes in v1:
time: 508 us; the launch traced here: 507 us
  waiting for transfers between devices  236 us (46%)
  blocking collectives  103 us (20%)
  matrix products  76.7 us (15%)
  local copies, waits for them, and re-layouts  74 us (15%)
  between operations  14.1 us (3%)
    all_to_all x1, blocking collectives, gather_by_exchange(): return lax.all_to_all(copies, axis, dim, dim, tiled=True)  103 us
    reduce_scatter x1, waiting for transfers between devices, local(): lax.psum_scatter(summed_rows.reshape(own_rows * lax.axis_size('seq'), 2 *...  82.2 us
    reduce_scatter x1, waiting for transfers between devices, local(): lax.psum_scatter(jnp.einsum('rf,rc->fc', full_states, own_grad, preferred...  66.1 us
    all_gather x1, waiting for transfers between devices, local(): lax.all_gather(own_values, 'seq', axis=0, tiled=True)  46.2 us
    all_gather x1, waiting for transfers between devices, local(): lax.all_gather(own_keys, 'seq', axis=0, tiled=True)  41.9 us
    dot_general x1, matrix products, local(): jnp.einsum('chqk,cqhd->ckhd', score_grad, queries_here, preferred_element...  17.6 us
    dot_general x1, matrix products, local(): jnp.einsum('chqk,ckhd->cqhd', score_grad, key_rows, preferred_element_typ...  14.7 us
    all_to_all x2, local copies, waits for them, and re-layouts, gather_by_exchange(): return lax.all_to_all(copies, axis, dim, dim, tiled=True)  12.8 us
  transfers between devices with their start and end apart: 4, of which 4 were waited for; matrix products, arithmetic and copies ran while one was open for 7% of the time, Pallas kernels for 0%

profile of v1, /device:TPU:2, one launch (start us, length us, event | category | flops | bytes accessed | tf_op | source)
XLA Modules:
  0.0 506.8 jit_solution(8786744350833485609)
XLA Ops:
  8.7 2.0 copy-done.4
  10.7 6.4 %copy.87 = bf16[256,16,512]{2,0,1:T(8,128)(2,1)} copy(bf16[256,16,512]{0,2,1:T(8,128)(2,1)} %bitcast.89) | data formatting | bytes 8388608 | tf_op jit(solution)/shard_map/all_to_all | solution.py:15
  17.1 103.3 %all_to_all.12 = bf16[256,16,512]{2,0,1:T(8,128)(2,1)} all-to-all(bf16[256,16,512]{2,0,1:T(8,128)(2,1)} %copy.87), channel_id=1, replica_groups=mesh['seq'=16,'head'=16] {'head'}, dimensions={1} | all-to-all | bytes 8388608 | tf_op jit(solution)/shard_map/all_to_all | solution.py:15
  120.5 6.4 %copy.88 = bf16[256,16,512]{0,2,1:T(8,128)(2,1)} copy(bf16[256,16,512]{2,0,1:T(8,128)(2,1)} %all_to_all.12) | data formatting | bytes 8388608 | tf_op jit(solution)/shard_map/all_to_all | solution.py:15
  126.8 5.4 %convolution_convert_fusion.1 = bf16[256,256]{1,0:T(8,128)(2,1)} fusion(bf16[256,8192]{0,1:T(8,128)(2,1)} %bitcast.85, bf16[8192,256]{1,0:T(8,128)(2,1)} %param.8), kind=kOutput, calls=%fused_computation.35 | convolution fusion | flops 1073807360 | bytes 8519680 | tf_op jit(solution)/shard_map/dot_general | solution.py:28
  132.4 5.5 %convolution_convert_fusion.2 = bf16[256,256]{1,0:T(8,128)(2,1)} fusion(bf16[256,8192]{0,1:T(8,128)(2,1)} %bitcast.86, bf16[8192,256]{1,0:T(8,128)(2,1)} %param.9), kind=kOutput, calls=%fused_computation.36 | convolution fusion | flops 1073807360 | bytes 8519680 | tf_op jit(solution)/shard_map/dot_general | solution.py:31
  138.8 41.9 %all-gather.5.cloned.1.call-done = bf16[4096,256]{1,0:T(8,128)(2,1)} async-done(((bf16[256,256]{1,0:T(8,128)(2,1)}), bf16[4096,256]{1,0:T(8,128)(2,1)}) %all-gather.5.cloned.1.call-update) | async-done | bytes 2097168 | tf_op jit(solution)/shard_map/all_gather | solution.py:35
  180.6 3.6 gather_fusion.1
  184.2 2.5 reshape.80
  186.8 46.2 %all-gather.3.cloned.1.call-done = bf16[4096,256]{1,0:T(8,128)(2,1)} async-done(((bf16[256,256]{1,0:T(8,128)(2,1)}), bf16[4096,256]{1,0:T(8,128)(2,1)}) %all-gather.3.cloned.1.call-update) | async-done | bytes 2097168 | tf_op jit(solution)/shard_map/all_gather | solution.py:36
  233.0 3.6 gather_fusion
  236.7 4.0 reshape.79
  241.5 2.0 fusion.63
  243.5 2.2 fusion.18
  245.6 8.5 %convolution_bitcast_fusion = f32[16,256,2,128]{3,1,2,0:T(8,128)} fusion(bf16[16,64,2,128]{3,2,1,0:T(2,128)(2,1)S(1)} %reshape.52, f32[16,2,64]{2,1,0:T(2,128)S(1)} %get-tuple-element.6, f32[16,2,256,64]{2,3,1,0:T(8,128)} %copy-done.3), kind=kOutput, calls=%fused_computation.11 | convolution fusion | flops 136841472 | bytes 6823936 | tf_op jit(solution)/shard_map/chqk,cqhd->ckhd/dot_general | solution.py:64
  254.1 17.6 %convolution_bitcast_fusion.1 = f32[16,256,2,128]{3,1,2,0:T(8,128)} fusion(f32[16,2,256,64]{2,3,1,0:T(8,128)} %fusion.18, bf16[16,64,2,128]{3,2,1,0:T(2,128)(2,1)S(1)} %reshape.50, f32[16,2,64,256]{3,2,1,0:T(8,128)} %get-tuple-element.7, f32[16,2,64]{2,1,0:T(2,128)S(1)} %get-tuple-element.6), kind=kOutput, calls=%fused_computation.12 | convolution fusion | flops 137890048 | bytes 8921088 | tf_op jit(solution)/shard_map/chqk,cqhd->ckhd/dot_general | solution.py:61
  271.7 5.5 %copy.102 = f32[16,256,2,128]{1,0,3,2:T(8,128)} copy(f32[16,256,2,128]{3,1,2,0:T(8,128)} %convolution_bitcast_fusion.1) | data formatting | bytes 8388608 | tf_op jit(solution)/shard_map/chqk,cqhd->ckhd/transpose | solution.py:61
  277.2 4.7 reshape.54
  282.0 5.6 %copy.105 = f32[32,128,256]{2,0,1:T(8,128)} copy(f32[32,128,256]{1,0,2:T(8,128)} %reshape.54) | data formatting | bytes 8388608 | tf_op jit(solution)/shard_map/reshape | solution.py:69
  287.6 5.5 %copy.104 = f32[16,256,2,128]{1,0,3,2:T(8,128)} copy(f32[16,256,2,128]{3,1,2,0:T(8,128)} %convolution_bitcast_fusion) | data formatting | bytes 8388608 | tf_op jit(solution)/shard_map/chqk,cqhd->ckhd/transpose | solution.py:64
  293.1 4.7 reshape.55
  297.8 5.6 %copy.106 = f32[32,128,256]{2,0,1:T(8,128)} copy(f32[32,128,256]{1,0,2:T(8,128)} %reshape.55) | data formatting | bytes 8388608 | tf_op jit(solution)/shard_map/reshape | solution.py:70
  303.4 4.8 fusion.3
  309.3 2.8 add_convert_fusion
  312.1 6.5 %copy.107 = bf16[32,128,512]{2,1,0:T(8,128)(2,1)} copy(bf16[32,128,512]{2,0,1:T(8,128)(2,1)} %add_convert_fusion) | data formatting | bytes 8388608 | tf_op jit(solution)/shard_map/convert_element_type | solution.py:86
  318.6 82.2 %reduce-scatter.3.cloned.1.call-done = bf16[256,512]{1,0:T(8,128)(2,1)} async-done(((bf16[4096,512]{1,0:T(8,128)(2,1)}), bf16[256,512]{1,0:T(8,128)(2,1)}) %reduce-scatter.3.cloned.1.call-update) | async-done | bytes 262160 | tf_op jit(solution)/shard_map/reduce_scatter | solution.py:85
  400.8 7.8 %convolution_convert_fusion = bf16[8192,512]{1,0:T(8,128)(2,1)} fusion(bf16[256,8192]{0,1:T(8,128)(2,1)} %bitcast.87, bf16[256,512]{1,0:T(8,128)(2,1)} %reduce-scatter.3.cloned.1.call-done), kind=kOutput, calls=%fused_computation.4 | convolution fusion | flops 2151677952 | bytes 12845056 | tf_op jit(solution)/shard_map/rf,rc->fc/dot_general | solution.py:92
  408.6 14.7 %fusion.28 = bf16[16,64,2,128]{3,1,2,0:T(8,128)(2,1)S(1)} fusion(bf16[16,256,2,128]{3,2,1,0:T(2,128)(2,1)S(1)} %reshape.80, f32[16,2,256,64]{2,3,1,0:T(8,128)} %fusion.18, f32[16,2,64,256]{3,2,1,0:T(8,128)} %get-tuple-element.7, f32[16,2,64]{2,1,0:T(2,128)S(1)} %get-tuple-element.6), kind=kOutput, calls=%fused_computation.33 | convolution fusion | flops 138152192 | bytes 6823936 | tf_op jit(solution)/shard_map/chqk,ckhd->cqhd/dot_general | solution.py:58
  423.9 6.6 %fusion.31 = bf16[16,64,2,128]{3,1,2,0:T(8,128)(2,1)S(1)} fusion(bf16[16,256,2,128]{3,2,1,0:T(2,128)(2,1)} %reshape.79, f32[16,2,64]{2,1,0:T(2,128)S(1)} %get-tuple-element.6, f32[16,2,256,64]{2,3,1,0:T(8,128)} %copy-done.3), kind=kOutput, calls=%fused_computation.34 | convolution fusion | flops 137103616 | bytes 4726784 | tf_op jit(solution)/shard_map/chqk,ckhd->cqhd/dot_general | solution.py:50
  431.0 1.1 copy_bitcast_fusion
  432.1 66.1 %reduce-scatter.5.cloned.1.call-done = bf16[512,512]{1,0:T(8,128)(2,1)} async-done(((bf16[8192,512]{1,0:T(8,128)(2,1)}), bf16[512,512]{1,0:T(8,128)(2,1)}) %reduce-scatter.5.cloned.1.call-update) | async-done | bytes 524304 | tf_op jit(solution)/shard_map/reduce_scatter | solution.py:91
  498.2 2.1 fusion.62
  (51 shorter events, 5.5 us)
Async XLA Ops:
  7.2 173.5 %all-gather.5.cloned.1.call-start = ((), (), s32[]{:S(2)}) async-start(), calls=%async_computation.4 | async-start | bytes 2228224 | tf_op jit(solution)/shard_map/all_gather | solution.py:35
  8.7 2.0 copy-start.4
  132.3 5.8 %copy-start.7 = (s32[16,2]{0,1:T(2,128)S(1)}, s32[16,2]{0,1:T(2,128)}, u32[]{:S(2)}) copy-start(s32[16,2]{0,1:T(2,128)} %param.10) | copy-start | bytes 388
  132.3 6.2 %copy-start.5 = (bf16[1024,256]{1,0:T(8,128)(2,1)S(1)}, bf16[1024,256]{1,0:T(8,128)(2,1)}, u32[]{:S(2)}) copy-start(bf16[1024,256]{1,0:T(8,128)(2,1)} %param.6) | copy-start | bytes 1572868
  132.3 6.3 %copy-start.6 = (bf16[1024,256]{1,0:T(8,128)(2,1)S(1)}, bf16[1024,256]{1,0:T(8,128)(2,1)}, u32[]{:S(2)}) copy-start(bf16[1024,256]{1,0:T(8,128)(2,1)} %param.11) | copy-start | bytes 1572868
  132.3 100.7 %all-gather.3.cloned.1.call-start = ((), (), s32[]{:S(2)}) async-start(), calls=%async_computation.3 | async-start | bytes 2228224 | tf_op jit(solution)/shard_map/all_gather | solution.py:36
  137.9 263.0 %reduce-scatter.3.cloned.1.call-start = ((), (), s32[]{:S(2)}) async-start(), calls=%async_computation.5 | async-start | bytes 4456448 | tf_op jit(solution)/shard_map/reduce_scatter | solution.py:85
  240.6 2.8 copy-start.2
  241.5 4.2 copy-start.3
  303.4 4.8 copy-start
  303.4 5.9 %copy-start.1 = (f32[32,128,256]{2,0,1:T(8,128)S(1)}, f32[32,128,256]{2,0,1:T(8,128)}, u32[]{:S(2)}) copy-start(f32[32,128,256]{2,0,1:T(8,128)} %copy.106) | copy-start | bytes 12582916
  318.6 179.6 %reduce-scatter.5.cloned.1.call-start = ((), (), s32[]{:S(2)}) async-start(), calls=%async_computation.6 | async-start | bytes 8912896 | tf_op jit(solution)/shard_map/reduce_scatter | solution.py:91
Sparse Core Ops, SparseCore 0:
  132.4 48.1 all-gather.4
  183.6 49.3 all-gather.2
  318.7 82.0 reduce-scatter.2
  408.8 89.4 reduce-scatter.4
